TPU v7x, 32 devices: a whole 2x2x4 slice. The times are simulated.
32 devices in a mesh: groups: 2 (over y), tm: 16 (over z, x, core).
Axes of the slice: x: 2, y: 2, z: 4, core: 2. Of those that a mesh axis runs over, the one named last changes fastest.
Arguments:
- start_frames: float32 [6, 4, 8, 256], P('groups'), parts along dimension 0, may hold values from -6 to 6
- plan: int32 [32], P(('groups', 'tm')), parts along dimension 0, may hold values from 0 to 999
- noise: float32 [16, 6, 4, 8, 256], P('tm', 'groups'), parts along dimension 1, may hold values from -6 to 6
- w_lift: float32 [3, 128], replicated, may hold values from -3.5 to 3.5
- w_time: float32 [128, 128], replicated, may hold values from -0.75 to 0.75
- spatial: float32 [2, 128, 9], replicated, may hold values from -2 to 2
- temporal: float32 [2, 128, 3], replicated, may hold values from -3.5 to 3.5
- w_point: bfloat16 [2, 128, 128], replicated, may hold values from -0.5 to 0.5
- w_out: float32 [128, 3], replicated, may hold values from -0.5 to 0.5
Outputs:
- trajectory: float32 [16, 6, 4, 8, 256], P('tm', 'groups'), parts along dimension 1
There are 2 independent parts, one for each index of `groups`. A program takes and returns all parts, laid end to end along the dimension named above; an argument that names none is the same for every part. Nothing has to cross between parts.
All inputs are finite; a program needn't handle non-finite values.
Results may differ from a plain program's by a relative error of at most 0.0023.
Values sent between devices are 32-bit elements; how exact they have to be, the bound alone decides.
A program may use at most 64 MiB of HBM per device.

v0:
```python
import functools
import math

import jax
import jax.numpy as jnp
from jax import lax
from jax.experimental import pallas as pl
from jax.experimental.pallas import tpu as pltpu
from jax.sharding import PartitionSpec as P

ITERS = 2
NOISE_SCALE = 2.0
MESH = pl.DeviceIdType.MESH
LANES = 128
HALO = 8
TILE_W = 16


def embedding(step_index, width):
    half_width = width // 2
    column = jnp.arange(half_width, dtype=jnp.float32)
    freqs = jnp.exp(-math.log(1000.0) * column / half_width)
    angles = step_index.astype(jnp.float32) * freqs
    return jnp.concatenate([jnp.sin(angles), jnp.cos(angles)])


def split_bf16(value):
    high = value.astype(jnp.bfloat16).astype(jnp.float32)
    return high, value - high


def kernel(
    n, share,
    start_ref, noise_ref, bias_ref, lift_ref, spatial_ref, temporal_ref, point_ref, wout_ref,
    out_ref,
    feat_a, feat_b, cols, lift_w, value, sent, got, sums, before,
    send_sem, recv_sem,
):
    channels, frames, rows, width = start_ref.shape
    hid = point_ref.shape[1]
    blocks = point_ref.shape[0]
    halves = width // LANES
    step_size = 1.0 / n
    me = lax.axis_index("tm")

    barrier = pltpu.get_barrier_semaphore()

    @pl.loop(1, n)
    def _(k):
        pl.semaphore_signal(
            barrier, inc=1, device_id={"tm": lax.rem(me + k, n)}, device_id_type=MESH
        )

    for feat in (feat_a, feat_b):
        zeros = jnp.zeros((frames * rows, HALO, hid), jnp.float32)
        feat[:, 0:HALO, :] = zeros
        feat[:, HALO + width : HALO + width + HALO, :] = zeros
    cols[...] = jnp.zeros_like(cols)
    cols[:, channels : channels + 1, :] = jnp.ones((frames * rows, 1, width), jnp.float32)
    lift_w[...] = jnp.zeros_like(lift_w)
    high, low = split_bf16(lift_ref[...])
    lift_w[0:channels, :] = high
    lift_w[8 : 8 + channels, :] = high
    lift_w[16 : 16 + channels, :] = low
    high, low = split_bf16(bias_ref[...])
    lift_w[channels : channels + 1, :] = high
    lift_w[16 + channels : 17 + channels, :] = low
    owned = frames * halves * rows // share
    for it in range(ITERS):
        if owned < n:
            sent[it, owned:n] = jnp.zeros((n - owned, channels, share, LANES), jnp.float32)

    def one_block(source, target, block):
        mean_w = jnp.full((hid, hid), 1.0 / hid, jnp.bfloat16)

        @pl.loop(0, width // TILE_W)
        def _(tile):
            w0 = pl.multiple_of(tile * TILE_W, TILE_W)
            taps = [spatial_ref[block, k : k + 1, :] for k in range(9)]
            times = [temporal_ref[block, k : k + 1, :] for k in range(3)]
            mixed = [[None] * rows for _ in range(frames)]
            acc = [[None] * rows for _ in range(frames)]
            for row in range(rows + 1):
                if row < rows:
                    for frame in range(frames):
                        at = frame * rows + row
                        cells = [source[at, pl.ds(w0 + HALO - 1 + c, TILE_W), :] for c in range(3)]
                        for tap in range(3):
                            to = row + 1 - tap
                            if 0 <= to < rows:
                                part = (
                                    taps[3 * tap] * cells[0]
                                    + taps[3 * tap + 1] * cells[1]
                                    + taps[3 * tap + 2] * cells[2]
                                )
                                old = acc[frame][to]
                                acc[frame][to] = part if old is None else old + part
                done = row - 1
                if done >= 0:
                    for frame in range(frames):
                        total = times[1] * acc[frame][done]
                        if frame > 0:
                            total = total + times[0] * acc[frame - 1][done]
                        if frame + 1 < frames:
                            total = total + times[2] * acc[frame + 1][done]
                        mixed[frame][done] = total
            flat = jnp.concatenate([m for per_frame in mixed for m in per_frame], axis=0)
            square = (flat * flat).astype(jnp.bfloat16)
            mean = jnp.dot(square, mean_w, preferred_element_type=jnp.float32)
            half = flat * lax.rsqrt(mean + 1e-06) * 0.5
            normed = (half * jnp.tanh(half) + half).astype(jnp.bfloat16)
            update = jnp.dot(normed, point_ref[block], preferred_element_type=jnp.float32)
            for at in range(frames * rows):
                here = pl.ds(w0 + HALO, TILE_W)
                fresh = source[at, here, :] + update[at * TILE_W : (at + 1) * TILE_W]
                target[at, here, :] = fresh.astype(jnp.bfloat16).astype(jnp.float32)

    def network():
        lift_weights = lift_w[...].astype(jnp.bfloat16)

        @pl.loop(0, frames * rows)
        def _(at):
            state = cols[at]
            high, low = split_bf16(state)
            left = jnp.concatenate([high, low, high, jnp.zeros_like(high)], axis=0)
            lifted = lax.dot_general(
                left.astype(jnp.bfloat16), lift_weights, (((0,), (0,)), ((), ())),
                preferred_element_type=jnp.float32,
            )
            feat_a[at, HALO : HALO + width, :] = lifted.astype(jnp.bfloat16).astype(jnp.float32)

        refs = (feat_a, feat_b)
        for block in range(blocks):
            one_block(refs[block % 2], refs[(block + 1) % 2], block)
        last = refs[blocks % 2]
        for at in range(frames * rows):
            frame, row = divmod(at, rows)
            cells = last[at, HALO : HALO + width, :].astype(jnp.bfloat16)
            both = lax.dot_general(
                wout_ref[...], cells, (((1,), (1,)), ((), ())), preferred_element_type=jnp.float32
            )
            result = both[0:8] + both[8:16]
            for channel in range(channels):
                for part in range(halves):
                    value[channel, frame * halves + part, row : row + 1, :] = result[
                        channel : channel + 1, part * LANES : (part + 1) * LANES
                    ]

    def groups(tile):
        size = share if rows % share == 0 else 1
        for first in range(0, rows, size):
            at = tile * rows + first
            yield at // share, at % share, first, size

    def copy_out(it, peer):
        return pltpu.make_async_remote_copy(
            src_ref=sent.at[it, peer], dst_ref=got.at[it, me],
            send_sem=send_sem.at[it, 0, peer], recv_sem=recv_sem.at[it, 0, me],
            device_id={"tm": peer}, device_id_type=MESH,
        )

    def copy_in(it, peer):
        return pltpu.make_async_remote_copy(
            src_ref=sent.at[it, peer], dst_ref=got.at[it, peer],
            send_sem=send_sem.at[it, 0, peer], recv_sem=recv_sem.at[it, 0, peer],
            device_id={"tm": peer}, device_id_type=MESH,
        )

    def back_out(it, peer):
        return pltpu.make_async_remote_copy(
            src_ref=sums.at[it, peer], dst_ref=before.at[it, me],
            send_sem=send_sem.at[it, 1, peer], recv_sem=recv_sem.at[it, 1, me],
            device_id={"tm": peer}, device_id_type=MESH,
        )

    def back_in(it, peer):
        return pltpu.make_async_remote_copy(
            src_ref=sums.at[it, peer], dst_ref=before.at[it, peer],
            send_sem=send_sem.at[it, 1, peer], recv_sem=recv_sem.at[it, 1, peer],
            device_id={"tm": peer}, device_id_type=MESH,
        )

    for it in range(ITERS):
        for channel in range(channels):
            for frame in range(frames):
                for part in range(halves):
                    lanes = slice(part * LANES, (part + 1) * LANES)
                    state = start_ref[channel, frame, :, lanes]
                    tile = frame * halves + part
                    if it > 0:
                        shift = [
                            before[it - 1, owner, channel, slot : slot + size, :]
                            for owner, slot, first, size in groups(tile)
                        ]
                        state = state + jnp.concatenate(shift, axis=0)
                    for row in range(rows):
                        cols[frame * rows + row, channel : channel + 1, lanes] = state[row : row + 1]
        network()
        for channel in range(channels):
            for frame in range(frames):
                for part in range(halves):
                    lanes = slice(part * LANES, (part + 1) * LANES)
                    tile = frame * halves + part
                    drift = (
                        step_size * value[channel, tile]
                        + NOISE_SCALE * math.sqrt(step_size) * noise_ref[channel, frame, :, lanes]
                    )
                    value[channel, tile] = drift
                    for owner, slot, first, size in groups(tile):
                        sent[it, owner, channel, slot : slot + size, :] = drift[first : first + size]
        if it == 0:
            pl.semaphore_wait(barrier, n - 1)

        @pl.loop(1, n)
        def _(k):
            copy_out(it, lax.rem(me + k, n)).start()

        got[it, me] = sent[it, me]

        def advance(peer, running):
            sums[it, peer] = running

            @pl.when(peer != me)
            def _():
                back_out(it, peer).start()
                copy_in(it, peer).wait_recv()

            return running + got[it, peer]

        lax.fori_loop(0, n, advance, jnp.zeros((channels, share, LANES), jnp.float32))
        before[it, me] = sums[it, me]

        @pl.loop(1, n)
        def _(k):
            peer = lax.rem(me + k, n)
            back_in(it, peer).wait_recv()
            copy_out(it, peer).wait_send()
            back_out(it, peer).wait_send()

    it = ITERS - 1
    for channel in range(channels):
        for frame in range(frames):
            for part in range(halves):
                lanes = slice(part * LANES, (part + 1) * LANES)
                tile = frame * halves + part
                shift = jnp.concatenate(
                    [
                        before[it, owner, channel, slot : slot + size, :]
                        for owner, slot, first, size in groups(tile)
                    ],
                    axis=0,
                )
                out_ref[channel, frame, :, lanes] = (
                    start_ref[channel, frame, :, lanes] + shift + value[channel, tile]
                )


def shards(start_frames, plan, noise, w_lift, w_time, spatial, temporal, w_point, w_out):
    n = lax.axis_size("tm")
    channels, frames, rows, width = start_frames.shape
    hid = w_time.shape[0]
    bias = jnp.dot(embedding(plan[0], hid)[None], w_time, precision=lax.Precision.HIGHEST)
    out_high = lax.reduce_precision(w_out.T, 8, 7)
    out_low = w_out.T - out_high
    pad = ((0, 8 - channels), (0, 0))
    wout = jnp.concatenate([jnp.pad(out_high, pad), jnp.pad(out_low, pad)]).astype(jnp.bfloat16)
    tiles = frames * (width // LANES)
    share = -(-tiles * rows // n)
    vmem = pl.BlockSpec(memory_space=pltpu.VMEM)
    exchange = pltpu.VMEM((ITERS, n, channels, share, LANES), jnp.float32)
    features = pltpu.VMEM((frames * rows, width + 2 * HALO, hid), jnp.float32)
    result = pl.pallas_call(
        functools.partial(kernel, n, share),
        out_shape=jax.ShapeDtypeStruct(start_frames.shape, jnp.float32),
        in_specs=[vmem] * 8,
        out_specs=vmem,
        scratch_shapes=[
            features,
            features,
            pltpu.VMEM((frames * rows, 8, width), jnp.float32),
            pltpu.VMEM((32, hid), jnp.float32),
            pltpu.VMEM((channels, tiles, rows, LANES), jnp.float32),
            exchange,
            exchange,
            exchange,
            exchange,
            pltpu.SemaphoreType.DMA((ITERS, 2, n)),
            pltpu.SemaphoreType.DMA((ITERS, 2, n)),
        ],
        compiler_params=pltpu.CompilerParams(
            collective_id=0, has_side_effects=True, vmem_limit_bytes=48 * 2**20
        ),
    )(
        start_frames, noise[0], bias, w_lift,
        spatial.transpose(0, 2, 1), temporal.transpose(0, 2, 1), w_point, wout,
    )
    return result[None]


def solution(mesh):
    in_specs = (
        P("groups", None, None, None),
        P(("groups", "tm")),
        P("tm", "groups", None, None, None),
        P(),
        P(),
        P(),
        P(),
        P(),
        P(),
    )
    out_specs = P("tm", "groups", None, None, None)
    return jax.shard_map(shards, mesh=mesh, in_specs=in_specs, out_specs=out_specs, check_vma=False)
```

profile of v0, /device:TPU:1, one launch (start us, length us, event | category | flops | bytes accessed | tf_op | source)
XLA Modules:
  0.0 67.7 jit_solution(5972051846028465823)
XLA Ops:
  0.0 0.0 copy-start
  0.0 0.0 copy-start.1
  0.7 0.1 copy-done
  0.8 0.2 fusion.4.bias_ref
  1.1 0.7 %reduce-precision_convert_fusion = (bf16[3,128]{1,0:T(4,128)(2,1)S(1)}, bf16[3,128]{1,0:T(4,128)(2,1)S(1)}) fusion(f32[128,3]{0,1:T(4,128)} %param.17), kind=kLoop, calls=%fused_computation.8 | loop fusion | flops 1536 | bytes 3072 | tf_op jit(solution)/shard_map/convert.4
  1.8 0.7 %copy.15 = f32[2,128,3]{1,2,0:T(4,128)S(1)} copy(f32[2,128,3]{1,0,2:T(2,128)} %param.15) | data formatting | bytes 6144 | tf_op args[6]
  2.5 0.0 copy-start.4
  2.5 0.7 %copy.14 = f32[2,128,9]{1,2,0:T(8,128)S(1)} copy(f32[2,128,9]{1,0,2:T(2,128)} %param.14) | data formatting | bytes 18432 | tf_op args[5]
  3.2 0.0 copy-done.1
  3.2 0.0 copy-done.4
  3.2 0.0 copy-start.2
  3.2 0.9 %copy-done.2 = f32[1,3,4,8,256]{4,3,2,1,0:T(8,128)S(1)} copy-done((f32[1,3,4,8,256]{4,3,2,1,0:T(8,128)S(1)}, f32[1,3,4,8,256]{4,3,2,1,0:T(8,128)}, u32[]{:S(2)}) %copy-start.2) | copy-done | bytes 98328
  4.1 0.0 copy-start.3
  4.1 0.8 %copy-done.3 = bf16[2,128,128]{2,1,0:T(8,128)(2,1)S(1)} copy-done((bf16[2,128,128]{2,1,0:T(8,128)(2,1)S(1)}, bf16[2,128,128]{2,1,0:T(8,128)(2,1)}, u32[]{:S(2)}) %copy-start.3) | copy-done | bytes 65560
  4.9 62.1 %shard_map.91 = f32[3,4,8,256]{3,2,1,0:T(8,128)S(1)} custom-call(f32[3,4,8,256]{3,2,1,0:T(8,128)S(1)} %copy-done.1, f32[3,4,8,256]{3,2,1,0:T(8,128)S(1)} %bitcast.18, f32[1,128]{1,0:T(1,128)S(1)} %fusion.4.bias_ref, f32[3,128]{1,0:T(4,128)S(1)} %copy-done.4, f32[2,9,128]{2,1,0:T(8,128)S(1)} %bitcast.19, f32[2,3,128]{2,1,0:T(4,128)S(1)} %bitcast.20, ...), custom_call_target="tpu_custom_call" | custom-call | tf_op jit(solution)/shard_map/pallas_call | solution.py:272
  67.0 0.6 copy.18
  (2 shorter events, 0.1 us)
Async XLA Ops:
  0.0 0.8 %copy-start = (f32[128,128]{1,0:T(8,128)S(1)}, f32[128,128]{1,0:T(8,128)}, u32[]{:S(2)}) copy-start(f32[128,128]{1,0:T(8,128)} %param.13) | copy-start | bytes 196612
  0.0 3.2 %copy-start.1 = (f32[3,4,8,256]{3,2,1,0:T(8,128)S(1)}, f32[3,4,8,256]{3,2,1,0:T(8,128)}, u32[]{:S(2)}) copy-start(f32[3,4,8,256]{3,2,1,0:T(8,128)} %start_ref.1) | copy-start | bytes 294916
  2.5 0.7 %copy-start.4 = (f32[3,128]{1,0:T(4,128)S(1)}, f32[3,128]{1,0:T(4,128)}, u32[]{:S(2)}) copy-start(f32[3,128]{1,0:T(4,128)} %lift_ref.1) | copy-start | bytes 4612
  3.2 0.9 %copy-start.2 = (f32[1,3,4,8,256]{4,3,2,1,0:T(8,128)S(1)}, f32[1,3,4,8,256]{4,3,2,1,0:T(8,128)}, u32[]{:S(2)}) copy-start(f32[1,3,4,8,256]{4,3,2,1,0:T(8,128)} %param.11) | copy-start | bytes 294916
  4.1 0.8 %copy-start.3 = (bf16[2,128,128]{2,1,0:T(8,128)(2,1)S(1)}, bf16[2,128,128]{2,1,0:T(8,128)(2,1)}, u32[]{:S(2)}) copy-start(bf16[2,128,128]{2,1,0:T(8,128)(2,1)} %point_ref.1) | copy-start | bytes 196612
where the time goes:
time: 68 us; the launch traced here: 67.7 us
  Pallas kernels  62.1 us (91%)
  local copies, waits for them, and re-layouts  3.88 us (6%)
  other arithmetic  0.76 us (1%)
  between operations  0.71 us (1%)
    pallas_call x1, Pallas kernels, shards(): pl.pallas_call(functools.partial(kernel, n, share), out_shape=jax.ShapeDt...  62.1 us
    unnamed x13, local copies, waits for them, and re-layouts  3.88 us

commit v1 on v0

--- a/solution.py
+++ b/solution.py
@@ -13,7 +13,7 @@
 MESH = pl.DeviceIdType.MESH
 LANES = 128
 HALO = 8
-TILE_W = 16
+TILE_W = 32
 
 
 def embedding(step_index, width):
@@ -33,7 +33,7 @@
     n, share,
     start_ref, noise_ref, bias_ref, lift_ref, spatial_ref, temporal_ref, point_ref, wout_ref,
     out_ref,
-    feat_a, feat_b, cols, lift_w, value, sent, got, sums, before,
+    feat_a, feat_b, cols, lift_w, out_w, conv_w, both_w, pending, value, sent, got, sums, before,
     send_sem, recv_sem,
 ):
     channels, frames, rows, width = start_ref.shape
@@ -62,6 +62,10 @@
     lift_w[0:channels, :] = high
     lift_w[8 : 8 + channels, :] = high
     lift_w[16 : 16 + channels, :] = low
+    out_w[...] = jnp.zeros_like(out_w)
+    high, low = split_bf16(wout_ref[...])
+    out_w[0:channels, :] = high
+    out_w[8 : 8 + channels, :] = low
     high, low = split_bf16(bias_ref[...])
     lift_w[channels : channels + 1, :] = high
     lift_w[16 + channels : 17 + channels, :] = low
@@ -70,55 +74,96 @@
         if owned < n:
             sent[it, owned:n] = jnp.zeros((n - owned, channels, share, LANES), jnp.float32)
 
+    spot = lax.broadcasted_iota(jnp.int32, (hid, hid), 0)
+    diagonal = spot == lax.broadcasted_iota(jnp.int32, (hid, hid), 1)
+    nothing = jnp.zeros((hid, hid), jnp.bfloat16)
+    both_w[...] = jnp.zeros_like(both_w)
+    for out in range(2):
+        here = slice(out * hid, (out + 1) * hid)
+        both_w[blocks, here, here] = jnp.full((hid, hid), 4.0 / hid, jnp.bfloat16)
+        for block in range(blocks):
+            both_w[block, here, here] = point_ref[block]
+            for near in range(4):
+                tap = near - out
+                for col in range(3):
+                    there = slice((3 * near + col) * hid, (3 * near + col + 1) * hid)
+                    if 0 <= tap < 3:
+                        k = 3 * tap + col
+                        weight = jnp.where(diagonal, spatial_ref[k, block : block + 1, :], 0.0)
+                        conv_w[block, there, here] = weight.astype(jnp.bfloat16)
+                    else:
+                        conv_w[block, there, here] = nothing
+
     def one_block(source, target, block):
-        mean_w = jnp.full((hid, hid), 1.0 / hid, jnp.bfloat16)
-
-        @pl.loop(0, width // TILE_W)
+        pairs = rows // 2
+        span = pairs * TILE_W
+
+        def convolve(tile):
+            w0 = pl.multiple_of(tile * TILE_W, TILE_W)
+            empty = jnp.zeros((TILE_W, hid), jnp.bfloat16)
+            stacked = []
+            for frame in range(frames):
+                cells = [[empty] * 3]
+                for row in range(rows):
+                    at = frame * rows + row
+                    cells.append([
+                        source[at, pl.ds(w0 + HALO - 1 + c, TILE_W), :].astype(jnp.bfloat16)
+                        for c in range(3)
+                    ])
+                cells.append([empty] * 3)
+                for pair in range(pairs):
+                    near = [cells[2 * pair + k][c] for k in range(4) for c in range(3)]
+                    stacked.append(jnp.concatenate(near, axis=1))
+            return jnp.dot(
+                jnp.concatenate(stacked, axis=0), conv_w[block], preferred_element_type=jnp.float32
+            )
+
+        def finish(tile, conv):
+            w0 = pl.multiple_of(tile * TILE_W, TILE_W)
+            times = []
+            for k in range(3):
+                weight = temporal_ref[k, block : block + 1, :]
+                times.append(jnp.concatenate([weight, weight], axis=1))
+            placed = [conv[frame * span : (frame + 1) * span] for frame in range(frames)]
+            mixed = []
+            for frame in range(frames):
+                total = times[1] * placed[frame]
+                if frame > 0:
+                    total = total + times[0] * placed[frame - 1]
+                if frame + 1 < frames:
+                    total = total + times[2] * placed[frame + 1]
+                mixed.append(total)
+            flat = jnp.concatenate(mixed, axis=0)
+            square = (flat * flat).astype(jnp.bfloat16)
+            mean = jnp.dot(square, both_w[blocks], preferred_element_type=jnp.float32)
+            half = flat * lax.rsqrt(mean + 4e-06)
+            normed = (half * jnp.tanh(half) + half).astype(jnp.bfloat16)
+            update = jnp.dot(normed, both_w[block], preferred_element_type=jnp.float32)
+            here = pl.ds(w0 + HALO, TILE_W)
+            for frame in range(frames):
+                for row in range(rows):
+                    at = frame * rows + row
+                    first = frame * span + (row // 2) * TILE_W
+                    out = row % 2
+                    part = update[first : first + TILE_W, out * hid : (out + 1) * hid]
+                    fresh = source[at, here, :] + part
+                    target[at, here, :] = fresh.astype(jnp.bfloat16).astype(jnp.float32)
+
+        tiles = width // TILE_W
+        pending[...] = convolve(0)
+
+        @pl.loop(1, tiles)
         def _(tile):
-            w0 = pl.multiple_of(tile * TILE_W, TILE_W)
-            taps = [spatial_ref[block, k : k + 1, :] for k in range(9)]
-            times = [temporal_ref[block, k : k + 1, :] for k in range(3)]
-            mixed = [[None] * rows for _ in range(frames)]
-            acc = [[None] * rows for _ in range(frames)]
-            for row in range(rows + 1):
-                if row < rows:
-                    for frame in range(frames):
-                        at = frame * rows + row
-                        cells = [source[at, pl.ds(w0 + HALO - 1 + c, TILE_W), :] for c in range(3)]
-                        for tap in range(3):
-                            to = row + 1 - tap
-                            if 0 <= to < rows:
-                                part = (
-                                    taps[3 * tap] * cells[0]
-                                    + taps[3 * tap + 1] * cells[1]
-                                    + taps[3 * tap + 2] * cells[2]
-                                )
-                                old = acc[frame][to]
-                                acc[frame][to] = part if old is None else old + part
-                done = row - 1
-                if done >= 0:
-                    for frame in range(frames):
-                        total = times[1] * acc[frame][done]
-                        if frame > 0:
-                            total = total + times[0] * acc[frame - 1][done]
-                        if frame + 1 < frames:
-                            total = total + times[2] * acc[frame + 1][done]
-                        mixed[frame][done] = total
-            flat = jnp.concatenate([m for per_frame in mixed for m in per_frame], axis=0)
-            square = (flat * flat).astype(jnp.bfloat16)
-            mean = jnp.dot(square, mean_w, preferred_element_type=jnp.float32)
-            half = flat * lax.rsqrt(mean + 1e-06) * 0.5
-            normed = (half * jnp.tanh(half) + half).astype(jnp.bfloat16)
-            update = jnp.dot(normed, point_ref[block], preferred_element_type=jnp.float32)
-            for at in range(frames * rows):
-                here = pl.ds(w0 + HALO, TILE_W)
-                fresh = source[at, here, :] + update[at * TILE_W : (at + 1) * TILE_W]
-                target[at, here, :] = fresh.astype(jnp.bfloat16).astype(jnp.float32)
+            earlier = pending[...]
+            pending[...] = convolve(tile)
+            finish(tile - 1, earlier)
+
+        finish(tiles - 1, pending[...])
 
     def network():
         lift_weights = lift_w[...].astype(jnp.bfloat16)
 
-        @pl.loop(0, frames * rows)
+        @pl.loop(0, frames * rows, unroll=4)
         def _(at):
             state = cols[at]
             high, low = split_bf16(state)
@@ -133,11 +178,12 @@
         for block in range(blocks):
             one_block(refs[block % 2], refs[(block + 1) % 2], block)
         last = refs[blocks % 2]
+        out_weights = out_w[...].astype(jnp.bfloat16)
         for at in range(frames * rows):
             frame, row = divmod(at, rows)
             cells = last[at, HALO : HALO + width, :].astype(jnp.bfloat16)
             both = lax.dot_general(
-                wout_ref[...], cells, (((1,), (1,)), ((), ())), preferred_element_type=jnp.float32
+                out_weights, cells, (((1,), (1,)), ((), ())), preferred_element_type=jnp.float32
             )
             result = both[0:8] + both[8:16]
             for channel in range(channels):
@@ -259,11 +305,8 @@
     n = lax.axis_size("tm")
     channels, frames, rows, width = start_frames.shape
     hid = w_time.shape[0]
+    blocks = spatial.shape[0]
     bias = jnp.dot(embedding(plan[0], hid)[None], w_time, precision=lax.Precision.HIGHEST)
-    out_high = lax.reduce_precision(w_out.T, 8, 7)
-    out_low = w_out.T - out_high
-    pad = ((0, 8 - channels), (0, 0))
-    wout = jnp.concatenate([jnp.pad(out_high, pad), jnp.pad(out_low, pad)]).astype(jnp.bfloat16)
     tiles = frames * (width // LANES)
     share = -(-tiles * rows // n)
     vmem = pl.BlockSpec(memory_space=pltpu.VMEM)
@@ -279,6 +322,10 @@
             features,
             pltpu.VMEM((frames * rows, 8, width), jnp.float32),
             pltpu.VMEM((32, hid), jnp.float32),
+            pltpu.VMEM((16, hid), jnp.float32),
+            pltpu.VMEM((blocks, 12 * hid, 2 * hid), jnp.bfloat16),
+            pltpu.VMEM((blocks + 1, 2 * hid, 2 * hid), jnp.bfloat16),
+            pltpu.VMEM((frames * rows // 2 * TILE_W, 2 * hid), jnp.float32),
             pltpu.VMEM((channels, tiles, rows, LANES), jnp.float32),
             exchange,
             exchange,
@@ -292,7 +339,7 @@
         ),
     )(
         start_frames, noise[0], bias, w_lift,
-        spatial.transpose(0, 2, 1), temporal.transpose(0, 2, 1), w_point, wout,
+        spatial.transpose(2, 0, 1), temporal.transpose(2, 0, 1), w_point, w_out.T,
     )
     return result[None]
 

time: 68 us -> 52 us (0.76)
  Pallas kernels: 62.1 us -> 47.8 us
  local copies, waits for them, and re-layouts: 3.88 us -> 3.04 us
  other arithmetic: 0.76 us -> 0.05 us
    pallas_call x1, Pallas kernels: 62.1 us -> 47.8 us  [shards(): pl.pallas_call(functools.partial(kernel, n, share), out_shape=jax.ShapeDt...]
    unnamed x13 -> x17, local copies, waits for them, and re-layouts: 3.88 us -> 3.04 us
    another operation x1 -> x0, other arithmetic: 0.7 us -> none
where the time goes in v1:
time: 52 us; the launch traced here: 51.8 us
  Pallas kernels  47.8 us (92%)
  local copies, waits for them, and re-layouts  3.04 us (6%)
  between operations  0.71 us (1%)
    pallas_call x1, Pallas kernels, shards(): pl.pallas_call(functools.partial(kernel, n, share), out_shape=jax.ShapeDt...  47.8 us
    unnamed x17, local copies, waits for them, and re-layouts  3.04 us

profile of v1, /device:TPU:1, one launch (start us, length us, event | category | flops | bytes accessed | tf_op | source)
XLA Modules:
  0.0 51.8 jit_solution(13558594976588470889)
XLA Ops:
  0.0 0.0 copy-start
  0.0 0.0 copy-start.3
  0.7 0.1 copy-done
  0.8 0.0 copy-start.4
  0.8 0.0 copy-start.5
  0.8 0.0 copy-start.6
  0.8 0.0 copy-start.7
  0.9 0.2 fusion.bias_ref
  1.1 0.0 copy-done.3
  1.1 0.5 copy-done.4
  1.5 0.0 copy-done.5
  1.6 0.0 copy-done.6
  1.6 0.0 copy-done.7
  1.6 0.0 copy-start.1
  1.6 0.9 %copy-done.1 = f32[3,4,8,256]{3,2,1,0:T(8,128)S(1)} copy-done((f32[3,4,8,256]{3,2,1,0:T(8,128)S(1)}, f32[3,4,8,256]{3,2,1,0:T(8,128)}, u32[]{:S(2)}) %copy-start.1) | copy-done | bytes 98328
  2.5 0.0 copy-start.2
  2.5 0.9 %copy-done.2 = f32[1,3,4,8,256]{4,3,2,1,0:T(8,128)S(1)} copy-done((f32[1,3,4,8,256]{4,3,2,1,0:T(8,128)S(1)}, f32[1,3,4,8,256]{4,3,2,1,0:T(8,128)}, u32[]{:S(2)}) %copy-start.2) | copy-done | bytes 98328
  3.4 47.8 %shard_map.91 = f32[3,4,8,256]{3,2,1,0:T(8,128)S(1)} custom-call(f32[3,4,8,256]{3,2,1,0:T(8,128)S(1)} %copy-done.1, f32[3,4,8,256]{3,2,1,0:T(8,128)S(1)} %bitcast.12, f32[1,128]{1,0:T(1,128)S(1)} %fusion.bias_ref, f32[3,128]{1,0:T(4,128)S(1)} %copy-done.6, f32[9,2,128]{2,1,0:T(2,128)S(1)} %bitcast.13, f32[3,2,128]{2,1,0:T(2,128)S(1)} %bitcast.14, ...), custom_call_target="tpu_custom_call" | custom-call | tf_op jit(solution)/shard_map/pallas_call | solution.py:315
  51.1 0.6 %copy.12 = f32[1,3,4,8,256]{4,3,2,1,0:T(8,128)} copy(f32[1,3,4,8,256]{4,3,2,1,0:T(8,128)S(1)} %bitcast.11) | data formatting | bytes 196608
  (1 shorter events, 0.0 us)
Async XLA Ops:
  0.0 0.8 %copy-start = (f32[128,128]{1,0:T(8,128)S(1)}, f32[128,128]{1,0:T(8,128)}, u32[]{:S(2)}) copy-start(f32[128,128]{1,0:T(8,128)} %param.13) | copy-start | bytes 196612
  0.0 1.1 %copy-start.3 = (bf16[2,128,128]{2,1,0:T(8,128)(2,1)S(1)}, bf16[2,128,128]{2,1,0:T(8,128)(2,1)}, u32[]{:S(2)}) copy-start(bf16[2,128,128]{2,1,0:T(8,128)(2,1)} %point_ref.1) | copy-start | bytes 196612
  0.8 0.7 %copy-start.4 = (f32[2,128,9]{1,0,2:T(2,128)S(1)}, f32[2,128,9]{1,0,2:T(2,128)}, u32[]{:S(2)}) copy-start(f32[2,128,9]{1,0,2:T(2,128)} %param.14) | copy-start | bytes 27652
  0.8 0.7 %copy-start.5 = (f32[2,128,3]{1,0,2:T(2,128)S(1)}, f32[2,128,3]{1,0,2:T(2,128)}, u32[]{:S(2)}) copy-start(f32[2,128,3]{1,0,2:T(2,128)} %param.15) | copy-start | bytes 9220
  0.8 0.7 %copy-start.6 = (f32[3,128]{1,0:T(4,128)S(1)}, f32[3,128]{1,0:T(4,128)}, u32[]{:S(2)}) copy-start(f32[3,128]{1,0:T(4,128)} %lift_ref.1) | copy-start | bytes 4612
  0.8 0.7 %copy-start.7 = (f32[128,3]{0,1:T(4,128)S(1)}, f32[128,3]{0,1:T(4,128)}, u32[]{:S(2)}) copy-start(f32[128,3]{0,1:T(4,128)} %param.17) | copy-start | bytes 4612
  1.6 0.9 %copy-start.1 = (f32[3,4,8,256]{3,2,1,0:T(8,128)S(1)}, f32[3,4,8,256]{3,2,1,0:T(8,128)}, u32[]{:S(2)}) copy-start(f32[3,4,8,256]{3,2,1,0:T(8,128)} %start_ref.1) | copy-start | bytes 294916
  2.5 0.9 %copy-start.2 = (f32[1,3,4,8,256]{4,3,2,1,0:T(8,128)S(1)}, f32[1,3,4,8,256]{4,3,2,1,0:T(8,128)}, u32[]{:S(2)}) copy-start(f32[1,3,4,8,256]{4,3,2,1,0:T(8,128)} %param.11) | copy-start | bytes 294916

commit v2 on v1

--- a/solution.py
+++ b/solution.py
@@ -76,23 +76,19 @@
 
     spot = lax.broadcasted_iota(jnp.int32, (hid, hid), 0)
     diagonal = spot == lax.broadcasted_iota(jnp.int32, (hid, hid), 1)
-    nothing = jnp.zeros((hid, hid), jnp.bfloat16)
     both_w[...] = jnp.zeros_like(both_w)
     for out in range(2):
         here = slice(out * hid, (out + 1) * hid)
         both_w[blocks, here, here] = jnp.full((hid, hid), 4.0 / hid, jnp.bfloat16)
         for block in range(blocks):
             both_w[block, here, here] = point_ref[block]
-            for near in range(4):
-                tap = near - out
+            for near in range(2):
+                tap = near + 1 - out
                 for col in range(3):
                     there = slice((3 * near + col) * hid, (3 * near + col + 1) * hid)
-                    if 0 <= tap < 3:
-                        k = 3 * tap + col
-                        weight = jnp.where(diagonal, spatial_ref[k, block : block + 1, :], 0.0)
-                        conv_w[block, there, here] = weight.astype(jnp.bfloat16)
-                    else:
-                        conv_w[block, there, here] = nothing
+                    k = 3 * tap + col
+                    weight = jnp.where(diagonal, spatial_ref[k, block : block + 1, :], 0.0)
+                    conv_w[block, there, here] = weight.astype(jnp.bfloat16)
 
     def one_block(source, target, block):
         pairs = rows // 2
@@ -100,19 +96,16 @@
 
         def convolve(tile):
             w0 = pl.multiple_of(tile * TILE_W, TILE_W)
-            empty = jnp.zeros((TILE_W, hid), jnp.bfloat16)
             stacked = []
             for frame in range(frames):
-                cells = [[empty] * 3]
-                for row in range(rows):
-                    at = frame * rows + row
-                    cells.append([
-                        source[at, pl.ds(w0 + HALO - 1 + c, TILE_W), :].astype(jnp.bfloat16)
+                for pair in range(pairs):
+                    near = [
+                        source[
+                            frame * rows + 2 * pair + k, pl.ds(w0 + HALO - 1 + c, TILE_W), :
+                        ].astype(jnp.bfloat16)
+                        for k in range(2)
                         for c in range(3)
-                    ])
-                cells.append([empty] * 3)
-                for pair in range(pairs):
-                    near = [cells[2 * pair + k][c] for k in range(4) for c in range(3)]
+                    ]
                     stacked.append(jnp.concatenate(near, axis=1))
             return jnp.dot(
                 jnp.concatenate(stacked, axis=0), conv_w[block], preferred_element_type=jnp.float32
@@ -124,7 +117,30 @@
             for k in range(3):
                 weight = temporal_ref[k, block : block + 1, :]
                 times.append(jnp.concatenate([weight, weight], axis=1))
-            placed = [conv[frame * span : (frame + 1) * span] for frame in range(frames)]
+
+            def outer(frame, row, tap):
+                parts = [
+                    spatial_ref[3 * tap + c, block : block + 1, :]
+                    * source[frame * rows + row, pl.ds(w0 + HALO - 1 + c, TILE_W), :]
+                    for c in range(3)
+                ]
+                return parts[0] + parts[1] + parts[2]
+
+            placed = []
+            for frame in range(frames):
+                for pair in range(pairs):
+                    first = frame * span + pair * TILE_W
+                    halves = []
+                    for out, row, tap in ((0, 2 * pair - 1, 0), (1, 2 * pair + 2, 2)):
+                        part = conv[first : first + TILE_W, out * hid : (out + 1) * hid]
+                        if 0 <= row < rows:
+                            part = part + outer(frame, row, tap)
+                        halves.append(part)
+                    placed.append(jnp.concatenate(halves, axis=1))
+            placed = [
+                jnp.concatenate(placed[frame * pairs : (frame + 1) * pairs], axis=0)
+                for frame in range(frames)
+            ]
             mixed = []
             for frame in range(frames):
                 total = times[1] * placed[frame]
@@ -134,9 +150,22 @@
                     total = total + times[2] * placed[frame + 1]
                 mixed.append(total)
             flat = jnp.concatenate(mixed, axis=0)
-            square = (flat * flat).astype(jnp.bfloat16)
-            mean = jnp.dot(square, both_w[blocks], preferred_element_type=jnp.float32)
-            half = flat * lax.rsqrt(mean + 4e-06)
+            square = flat * flat
+            scale = jnp.concatenate(
+                [
+                    jnp.broadcast_to(
+                        lax.rsqrt(
+                            jnp.sum(square[:, out * hid : (out + 1) * hid], axis=1, keepdims=True)
+                            * (4.0 / hid)
+                            + 4e-06
+                        ),
+                        (frames * span, hid),
+                    )
+                    for out in range(2)
+                ],
+                axis=1,
+            )
+            half = flat * scale
             normed = (half * jnp.tanh(half) + half).astype(jnp.bfloat16)
             update = jnp.dot(normed, both_w[block], preferred_element_type=jnp.float32)
             here = pl.ds(w0 + HALO, TILE_W)
@@ -323,7 +352,7 @@
             pltpu.VMEM((frames * rows, 8, width), jnp.float32),
             pltpu.VMEM((32, hid), jnp.float32),
             pltpu.VMEM((16, hid), jnp.float32),
-            pltpu.VMEM((blocks, 12 * hid, 2 * hid), jnp.bfloat16),
+            pltpu.VMEM((blocks, 6 * hid, 2 * hid), jnp.bfloat16),
             pltpu.VMEM((blocks + 1, 2 * hid, 2 * hid), jnp.bfloat16),
             pltpu.VMEM((frames * rows // 2 * TILE_W, 2 * hid), jnp.float32),
             pltpu.VMEM((channels, tiles, rows, LANES), jnp.float32),

time: 52 us -> 46.3 us (0.89)
  Pallas kernels: 47.8 us -> 42 us
    pallas_call x1, Pallas kernels: 47.8 us -> 42 us  [shards(): pl.pallas_call(functools.partial(kernel, n, share), out_shape=jax.ShapeDt...]
where the time goes in v2:
time: 46.3 us; the launch traced here: 46.1 us
  Pallas kernels  42 us (91%)
  local copies, waits for them, and re-layouts  3.04 us (7%)
  between operations  0.71 us (2%)
    pallas_call x1, Pallas kernels, shards(): pl.pallas_call(functools.partial(kernel, n, share), out_shape=jax.ShapeDt...  42 us
    unnamed x17, local copies, waits for them, and re-layouts  3.04 us

profile of v2, /device:TPU:1, one launch (start us, length us, event | category | flops | bytes accessed | tf_op | source)
XLA Modules:
  0.0 46.1 jit_solution(4070309772810165317)
XLA Ops:
  0.0 0.0 copy-start
  0.0 0.0 copy-start.3
  0.7 0.1 copy-done
  0.8 0.0 copy-start.4
  0.8 0.0 copy-start.5
  0.8 0.0 copy-start.6
  0.8 0.0 copy-start.7
  0.9 0.2 fusion.bias_ref
  1.1 0.0 copy-done.3
  1.1 0.5 %copy-done.4 = f32[2,128,9]{1,0,2:T(2,128)S(1)} copy-done((f32[2,128,9]{1,0,2:T(2,128)S(1)}, f32[2,128,9]{1,0,2:T(2,128)}, u32[]{:S(2)}) %copy-start.4) | copy-done | bytes 9240
  1.5 0.0 copy-done.5
  1.6 0.0 copy-done.6
  1.6 0.0 copy-done.7
  1.6 0.0 copy-start.1
  1.6 0.9 %copy-done.1 = f32[3,4,8,256]{3,2,1,0:T(8,128)S(1)} copy-done((f32[3,4,8,256]{3,2,1,0:T(8,128)S(1)}, f32[3,4,8,256]{3,2,1,0:T(8,128)}, u32[]{:S(2)}) %copy-start.1) | copy-done | bytes 98328
  2.5 0.0 copy-start.2
  2.5 0.9 %copy-done.2 = f32[1,3,4,8,256]{4,3,2,1,0:T(8,128)S(1)} copy-done((f32[1,3,4,8,256]{4,3,2,1,0:T(8,128)S(1)}, f32[1,3,4,8,256]{4,3,2,1,0:T(8,128)}, u32[]{:S(2)}) %copy-start.2) | copy-done | bytes 98328
  3.4 42.0 %shard_map.91 = f32[3,4,8,256]{3,2,1,0:T(8,128)S(1)} custom-call(f32[3,4,8,256]{3,2,1,0:T(8,128)S(1)} %copy-done.1, f32[3,4,8,256]{3,2,1,0:T(8,128)S(1)} %bitcast.12, f32[1,128]{1,0:T(1,128)S(1)} %fusion.bias_ref, f32[3,128]{1,0:T(4,128)S(1)} %copy-done.6, f32[9,2,128]{2,1,0:T(2,128)S(1)} %bitcast.13, f32[3,2,128]{2,1,0:T(2,128)S(1)} %bitcast.14, ...), custom_call_target="tpu_custom_call" | custom-call | tf_op jit(solution)/shard_map/pallas_call | solution.py:344
  45.4 0.6 %copy.12 = f32[1,3,4,8,256]{4,3,2,1,0:T(8,128)} copy(f32[1,3,4,8,256]{4,3,2,1,0:T(8,128)S(1)} %bitcast.11) | data formatting | bytes 196608
  (1 shorter events, 0.0 us)
Async XLA Ops:
  0.0 0.8 %copy-start = (f32[128,128]{1,0:T(8,128)S(1)}, f32[128,128]{1,0:T(8,128)}, u32[]{:S(2)}) copy-start(f32[128,128]{1,0:T(8,128)} %param.13) | copy-start | bytes 196612
  0.0 1.1 %copy-start.3 = (bf16[2,128,128]{2,1,0:T(8,128)(2,1)S(1)}, bf16[2,128,128]{2,1,0:T(8,128)(2,1)}, u32[]{:S(2)}) copy-start(bf16[2,128,128]{2,1,0:T(8,128)(2,1)} %point_ref.1) | copy-start | bytes 196612
  0.8 0.7 %copy-start.4 = (f32[2,128,9]{1,0,2:T(2,128)S(1)}, f32[2,128,9]{1,0,2:T(2,128)}, u32[]{:S(2)}) copy-start(f32[2,128,9]{1,0,2:T(2,128)} %param.14) | copy-start | bytes 27652
  0.8 0.7 %copy-start.5 = (f32[2,128,3]{1,0,2:T(2,128)S(1)}, f32[2,128,3]{1,0,2:T(2,128)}, u32[]{:S(2)}) copy-start(f32[2,128,3]{1,0,2:T(2,128)} %param.15) | copy-start | bytes 9220
  0.8 0.7 %copy-start.6 = (f32[3,128]{1,0:T(4,128)S(1)}, f32[3,128]{1,0:T(4,128)}, u32[]{:S(2)}) copy-start(f32[3,128]{1,0:T(4,128)} %lift_ref.1) | copy-start | bytes 4612
  0.8 0.7 %copy-start.7 = (f32[128,3]{0,1:T(4,128)S(1)}, f32[128,3]{0,1:T(4,128)}, u32[]{:S(2)}) copy-start(f32[128,3]{0,1:T(4,128)} %param.17) | copy-start | bytes 4612
  1.6 0.9 %copy-start.1 = (f32[3,4,8,256]{3,2,1,0:T(8,128)S(1)}, f32[3,4,8,256]{3,2,1,0:T(8,128)}, u32[]{:S(2)}) copy-start(f32[3,4,8,256]{3,2,1,0:T(8,128)} %start_ref.1) | copy-start | bytes 294916
  2.5 0.9 %copy-start.2 = (f32[1,3,4,8,256]{4,3,2,1,0:T(8,128)S(1)}, f32[1,3,4,8,256]{4,3,2,1,0:T(8,128)}, u32[]{:S(2)}) copy-start(f32[1,3,4,8,256]{4,3,2,1,0:T(8,128)} %param.11) | copy-start | bytes 294916
